TPU v7x, 32 devices: a whole 2x2x4 slice. The times are simulated.
32 devices in a mesh: depth: 8 (over y, x, core), group: 4 (over z).
Axes of the slice: x: 2, y: 2, z: 4, core: 2. Of those that a mesh axis runs over, the one named last changes fastest.
Arguments:
- output_one: bfloat16 [32, 128, 64, 128], P(None, 'depth', 'group'), may hold values from -6 to 6
- output_two: bfloat16 [32, 128, 64, 128], P(None, 'depth', 'group'), may hold values from -6 to 6
- cotangent_one: bfloat16 [32, 128, 64, 128], P(None, 'depth', 'group'), may hold values from -6 to 6
- cotangent_two: bfloat16 [32, 128, 64, 128], P(None, 'depth', 'group'), may hold values from -6 to 6
- first_weight: bfloat16 [27, 32, 32], replicated, may hold values from -0.21875 to 0.21875
- second_weight: bfloat16 [27, 32, 32], replicated, may hold values from -0.21875 to 0.21875
- bricks: int32 [8, 4, 8], P('depth'), may hold values from 0 to 8, as said below
Outputs:
- restored_one: bfloat16 [32, 128, 64, 128], P(None, 'depth', 'group')
- restored_two: bfloat16 [32, 128, 64, 128], P(None, 'depth', 'group')
- input_grad_one: bfloat16 [32, 128, 64, 128], P(None, 'depth', 'group')
- input_grad_two: bfloat16 [32, 128, 64, 128], P(None, 'depth', 'group')
- first_weight_grad: float32 [27, 32, 32], replicated
- second_weight_grad: float32 [27, 32, 32], replicated
Inputs may be any that keep to these rules, and one draw needn't show every extreme that they name: bricks[z, g, :] lists the positions of the occupied bricks of depth layer z and lateral row g, distinct and ascending, followed by 8 in every unused entry. For each z the numbers of occupied bricks over g = 0 .. 3 are a reordering of 1 + (7 * j * j) // 9 for j = 0 .. 3, so in every depth layer one row has all 8 bricks occupied and the layer holds at most 16 occupied bricks.
All inputs are finite; a program needn't handle non-finite values.
Results may differ from a plain program's by a relative error of at most 0.0085.
Values may be sent and summed in bfloat16 or wider, within the bound.
No kernel may reach another device: no remote copies, remote signals or barrier semaphores. Data moves between devices by JAX's collectives and lax.ppermute only.
A program may use at most 256 MiB of HBM per device.

v0:
```python
import math
import jax
import jax.numpy as jnp
from jax import lax
from jax.sharding import PartitionSpec as P


def extended_2(shard, sides, width):
    for axis, dim in sides:
        size, length = (lax.axis_size(axis), shard.shape[dim])
        up = [(i, (i + 1) % size) for i in range(size - 1)]
        down = [(j, i) for i, j in up]
        last = lax.slice_in_dim(shard, length - width, length, axis=dim)
        initial = lax.slice_in_dim(shard, 0, width, axis=dim)
        before = lax.ppermute(last, axis, up)
        after = lax.ppermute(initial, axis, down)
        shard = jnp.concatenate([before, shard, after], axis=dim)
    return shard


def logistic_slope(inputs):
    logistic = jax.nn.sigmoid(inputs)
    return logistic * (1.0 + inputs * (1.0 - logistic))


def tap_offsets(brick_edge):
    window_edge = brick_edge + 2
    offsets = []
    for depth_step in range(3):
        for row_step in range(3):
            for col_step in range(3):
                offsets.append(
                    depth_step * window_edge * window_edge + row_step * window_edge + col_step
                )
    return offsets


def grid_length(brick_edge):
    window_edge = brick_edge + 2
    return (
        (brick_edge - 1) * window_edge * window_edge + (brick_edge - 1) * window_edge + brick_edge
    )


def padded_length(brick_edge):
    return (grid_length(brick_edge) + 127) // 128 * 128


def extend(window, brick_edge):
    needed = max(tap_offsets(brick_edge)) + padded_length(brick_edge)
    return jnp.pad(window, ((0, 0), (0, max(needed - window.shape[1], 0))))


def convolve(window, kernel, brick_edge):
    length = padded_length(brick_edge)
    total = jnp.zeros((kernel.shape[1], length), jnp.float32)
    for number, offset in enumerate(tap_offsets(brick_edge)):
        total = total + jnp.dot(
            kernel[number], window[:, offset : offset + length], preferred_element_type=jnp.float32
        )
    return total


def grid_to_brick(values, brick_edge):
    window_edge = brick_edge + 2
    channels = values.shape[0]
    full_size = brick_edge * window_edge * window_edge
    values = values[:, : grid_length(brick_edge)]
    padded = jnp.pad(values, ((0, 0), (0, full_size - values.shape[1])))
    cubes = padded.reshape(channels, brick_edge, window_edge, window_edge)[
        :, :, :brick_edge, :brick_edge
    ]
    return cubes.reshape(channels, brick_edge**3)


def brick_to_grid(values, brick_edge):
    channels = values.shape[0]
    cubes = values.reshape(channels, brick_edge, brick_edge, brick_edge)
    padded = jnp.pad(cubes, ((0, 0), (0, 0), (0, 2), (0, 2)))
    grid = padded.reshape(channels, -1)[:, : grid_length(brick_edge)]
    return jnp.pad(grid, ((0, 0), (0, padded_length(brick_edge) - grid_length(brick_edge))))


def centre(window, brick_edge):
    window_edge = brick_edge + 2
    offset = window_edge * window_edge + window_edge + 1
    return grid_to_brick(window[:, offset : offset + grid_length(brick_edge)], brick_edge)


def weight_gradient(errors, window, brick_edge):
    grid = brick_to_grid(errors, brick_edge)
    length = padded_length(brick_edge)
    pieces = []
    for offset in tap_offsets(brick_edge):
        pieces.append(
            lax.dot_general(
                grid,
                window[:, offset : offset + length],
                (((1,), (1,)), ((), ())),
                preferred_element_type=jnp.float32,
            )
        )
    return jnp.stack(pieces, axis=0)


def first_round(windows, kernels, brick_edge):
    source = extend(windows[0], brick_edge)
    preact = grid_to_brick(convolve(source, kernels[1], brick_edge), brick_edge)
    cotangent = centre(windows[1], brick_edge).astype(jnp.float32)
    shaped = jax.nn.silu(preact).astype(jnp.bfloat16)
    errors = (cotangent * logistic_slope(preact)).astype(jnp.bfloat16)
    return (jnp.stack([shaped, errors]), weight_gradient(errors, source, brick_edge))


def second_round(windows, kernels, brick_edge):
    source = extend(windows[0], brick_edge)
    preact = grid_to_brick(convolve(source, kernels[0], brick_edge), brick_edge)
    spread = grid_to_brick(
        convolve(extend(windows[1], brick_edge), kernels[3], brick_edge), brick_edge
    )
    totals = (centre(windows[2], brick_edge).astype(jnp.float32) + spread).astype(jnp.bfloat16)
    shaped = jax.nn.silu(preact).astype(jnp.bfloat16)
    errors = (totals.astype(jnp.float32) * logistic_slope(preact)).astype(jnp.bfloat16)
    return (jnp.stack([totals, shaped, errors]), weight_gradient(errors, source, brick_edge))


def third_round(windows, kernels, brick_edge):
    spread = grid_to_brick(
        convolve(extend(windows[0], brick_edge), kernels[2], brick_edge), brick_edge
    )
    result = (centre(windows[1], brick_edge).astype(jnp.float32) + spread).astype(jnp.bfloat16)
    channels = result.shape[0]
    return (result[None], jnp.zeros((27, channels, channels), jnp.float32))


def cut_window(padded, offset, brick_edge):
    window_edge = brick_edge + 2
    anchor = jnp.zeros((), jnp.int32)
    block = lax.dynamic_slice(
        padded,
        (anchor, anchor, anchor, anchor, offset),
        (padded.shape[0], padded.shape[1], window_edge, window_edge, window_edge),
    )
    return block.reshape(padded.shape[0], padded.shape[1], window_edge**3)


def with_faces(stacked):
    extended = extended_2(stacked, (("depth", 2), ("group", 3)), 1)
    return jnp.pad(extended, ((0, 0), (0, 0), (0, 0), (0, 0), (1, 1)))


def zero_rim(volume):
    return jnp.pad(volume[None], ((0, 0), (0, 0), (1, 1), (1, 1), (1, 1)))


def own_pass(padded, initial, compute, own_list, own_count, brick_edge, grad_shape):

    def visit(number, state):
        slab_stack, partials = state
        offset = own_list[number] * brick_edge
        bricks_out, gradient = compute(cut_window(padded, offset, brick_edge))
        cubes = bricks_out.reshape(
            bricks_out.shape[0], bricks_out.shape[1], brick_edge, brick_edge, brick_edge
        )
        anchor = jnp.zeros((), jnp.int32)
        slab_stack = lax.dynamic_update_slice(
            slab_stack, cubes, (anchor, anchor, anchor, anchor, offset)
        )
        return (slab_stack, partials + gradient)

    return lax.fori_loop(0, own_count, visit, (initial, jnp.zeros(grad_shape, jnp.float32)))


def local(
    output_one, output_two, cotangent_one, cotangent_two, first_weight, second_weight, bricks
):
    brick_edge = output_one.shape[1]
    across = output_one.shape[3]
    slots = bricks.shape[2]
    groups = lax.axis_size("group")
    position = lax.axis_index("group")
    listing = bricks[0]
    counts = jnp.sum((listing < slots).astype(jnp.int32), axis=1)
    own_list = listing[position]
    own_count = counts[position]
    present = jnp.any(own_list[:, None] == jnp.arange(slots, dtype=jnp.int32)[None, :], axis=0)
    column_mask = jnp.repeat(present.astype(jnp.float32), brick_edge)
    kernels = (
        first_weight,
        second_weight,
        jnp.transpose(jnp.flip(first_weight, 0), (0, 2, 1)),
        jnp.transpose(jnp.flip(second_weight, 0), (0, 2, 1)),
    )
    grad_shape = first_weight.shape

    def run_round(padded, initial, compute):
        return own_pass(padded, initial, compute, own_list, own_count, brick_edge, grad_shape)

    zeros_volume = jnp.zeros_like(output_one)
    upper_masked = (output_one.astype(jnp.float32) * column_mask).astype(jnp.bfloat16)
    padded = jnp.concatenate([with_faces(upper_masked[None]), zero_rim(cotangent_two)], axis=0)
    first_stack, second_partial = run_round(
        padded,
        jnp.stack([zeros_volume, zeros_volume]),
        lambda windows: first_round(windows, kernels, brick_edge),
    )
    restored_two = (output_two.astype(jnp.float32) - first_stack[0].astype(jnp.float32)).astype(
        jnp.bfloat16
    )
    lower_masked = (restored_two.astype(jnp.float32) * column_mask).astype(jnp.bfloat16)
    padded = jnp.concatenate(
        [with_faces(jnp.stack([lower_masked, first_stack[1]])), zero_rim(cotangent_one)], axis=0
    )
    second_stack, first_partial = run_round(
        padded,
        jnp.stack([cotangent_one, zeros_volume, zeros_volume]),
        lambda windows: second_round(windows, kernels, brick_edge),
    )
    input_grad_one = second_stack[0]
    restored_one = (output_one.astype(jnp.float32) - second_stack[1].astype(jnp.float32)).astype(
        jnp.bfloat16
    )
    padded = jnp.concatenate([with_faces(second_stack[2][None]), zero_rim(cotangent_two)], axis=0)
    third_stack, unused = run_round(
        padded, cotangent_two[None], lambda windows: third_round(windows, kernels, brick_edge)
    )
    input_grad_two = third_stack[0]
    first_total, second_total = lax.psum((first_partial, second_partial), ("depth", "group"))
    scale = 1.0 / math.sqrt(
        float(brick_edge * lax.axis_size("depth") * brick_edge * groups * across)
    )
    return (
        restored_one,
        restored_two,
        input_grad_one,
        input_grad_two,
        first_total * scale,
        second_total * scale,
    )


def solution(mesh):
    placed = (
        P(None, "depth", "group", None),
        P(None, "depth", "group", None),
        P(None, "depth", "group", None),
        P(None, "depth", "group", None),
        P(),
        P(),
        P("depth", None, None),
    )
    return jax.shard_map(
        local,
        mesh=mesh,
        in_specs=placed,
        out_specs=(
            P(None, "depth", "group", None),
            P(None, "depth", "group", None),
            P(None, "depth", "group", None),
            P(None, "depth", "group", None),
            P(),
            P(),
        ),
        check_vma=False,
    )
```

profile of v0, /device:TPU:0, one launch (start us, length us, event | category | flops | bytes accessed | tf_op | source)
XLA Modules:
  0.0 2359.1 jit_solution(11144788152635191099)
XLA Ops:
  29.5 6.9 select_maximum_fusion.6
  36.4 9.6 fusion.928
  46.1 22.5 copy.67
  68.5 6.4 broadcast.173
  75.7 612.9 %while.40 = (s32[]{:T(128)}, bf16[2,32,16,16,128]{1,4,3,2,0:T(8,128)(2,1)}, f32[27,32,32]{2,1,0:T(8,128)}, s32[]{:T(128)}, s32[8]{0:T(128)S(1)}, /*index=5*/bf16...) while((s32[]{:T(128)}, ...), condition=%wide.region_3.4_spmd, body=%wide.region_2.3_spmd.sunk | while | flops 587555840 | bytes 164357712 | solution.py:171
  100.9 6.3 constant_dynamic-slice_fusion.10
  130.0 4.2 reshape.203
  173.7 6.3 constant_dynamic-slice_fusion.10
  246.5 6.3 constant_dynamic-slice_fusion.10
  319.2 6.3 constant_dynamic-slice_fusion.10
  392.0 6.3 constant_dynamic-slice_fusion.10
  464.7 6.3 constant_dynamic-slice_fusion.10
  537.5 6.3 constant_dynamic-slice_fusion.10
  610.3 5.9 constant_dynamic-slice_fusion.10
  688.6 15.1 copy.68
  715.4 7.9 collective-permute-start.6
  724.8 5.9 copy.79
  733.7 5.8 copy.84
  739.5 17.1 stack.360.clone
  763.0 14.0 select_maximum_fusion
  777.0 6.8 fusion.920
  783.9 33.0 %copy.72 = bf16[3,32,18,18,130]{1,4,3,2,0:T(8,128)(2,1)} copy(bf16[3,32,18,18,130]{4,1,3,2,0:T(8,128)(2,1)} %fusion.920) | data formatting | bytes 16174080 | tf_op jit(solution)/shard_map/while | solution.py:171
  817.7 965.3 %while.41 = (s32[]{:T(128)}, bf16[3,32,16,16,128]{1,4,3,2,0:T(8,128)(2,1)}, f32[27,32,32]{2,1,0:T(8,128)}, s32[]{:T(128)}, s32[8]{0:T(128)S(1)}, /*index=5*/bf16...) while((s32[]{:T(128)}, ...), condition=%wide.region_5.6_spmd, body=%wide.region_4.5_spmd.sunk | while | flops 883973120 | bytes 240212160 | solution.py:171
  819.9 8.9 constant_dynamic-slice_fusion.11
  892.3 4.3 reshape.208
  902.0 4.9 fusion.1743
  939.7 8.9 constant_dynamic-slice_fusion.11
  1012.0 4.3 reshape.208
  1021.6 4.9 fusion.1743
  1059.3 9.0 constant_dynamic-slice_fusion.11
  1131.6 4.3 reshape.208
  1141.3 4.9 fusion.1743
  1179.0 9.0 constant_dynamic-slice_fusion.11
  1251.3 4.3 reshape.208
  1260.9 4.9 fusion.1743
  1298.6 8.9 constant_dynamic-slice_fusion.11
  1370.8 4.3 reshape.208
  1380.5 4.9 fusion.1743
  1418.1 8.9 constant_dynamic-slice_fusion.11
  1490.4 4.3 reshape.208
  1500.1 4.9 fusion.1743
  1537.8 8.9 constant_dynamic-slice_fusion.11
  1610.0 4.3 reshape.208
  1619.7 4.9 fusion.1743
  1657.4 8.3 constant_dynamic-slice_fusion.11
  1729.1 4.3 reshape.208
  1738.8 4.9 fusion.1743
  1783.1 22.0 copy.73
  1806.1 4.4 fusion.937
  1810.4 23.4 copy.74
  1849.0 134.6 %all-reduce.20.cloned.1.call-done = (f32[27,32,32]{2,1,0:T(8,128)}, f32[27,32,32]{2,1,0:T(8,128)}) async-done(((f32[27,32,32]{2,1,0:T(8,128)}, f32[27,32,32]{2,1,0:T(8,128)}), (f32[27,32,32]{2,1,0:T(8,128)}, f32[27,32,32]{2,1,0:T(8,128)})) %all-reduce.20.cloned.1.call-update) | async-done | bytes 221200 | tf_op jit(solution)/shard_map/psum | solution.py:228
  1985.8 8.2 select_maximum_fusion.2
  1994.0 9.6 fusion.929
  2003.6 22.5 copy.80
  2026.1 317.2 %while.42 = (s32[]{:T(128)}, bf16[1,32,16,16,128]{1,4,3,2,0:T(8,128)(2,1)}, s32[]{:T(128)}, s32[8]{0:T(128)S(1)}, bf16[2,32,18,18,130]{1,4,3,2,0:T(8,128)(2,1)},...) while((s32[]{:T(128)}, ...), condition=%wide.region_7.8_spmd, body=%wide.region_6.7_spmd.sunk | while | flops 295106560 | bytes 87847184 | solution.py:171
  2028.2 6.3 constant_dynamic-slice_fusion.12
  2067.8 6.3 constant_dynamic-slice_fusion.12
  2107.3 6.3 constant_dynamic-slice_fusion.12
  2146.9 6.3 constant_dynamic-slice_fusion.12
  2186.4 6.3 constant_dynamic-slice_fusion.12
  2226.0 6.3 constant_dynamic-slice_fusion.12
  2265.5 6.3 constant_dynamic-slice_fusion.12
  2305.1 5.9 constant_dynamic-slice_fusion.12
  2343.3 8.6 copy.81
  (1905 shorter events, 1627.5 us)
Async XLA Ops:
  7.2 1976.5 %all-reduce.20.cloned.1.call-start = ((), (), s32[]{:S(2)}) async-start(), calls=%async_computation | async-start | bytes 1769472 | tf_op jit(solution)/shard_map/psum | solution.py:228
  8.2 3.0 copy-start.27
  11.1 7.8 copy-start.16
  11.2 3.7 collective-permute-start
  13.6 5.3 collective-permute-start.1
  19.0 8.8 collective-permute-start.2
  22.5 7.0 collective-permute-start.3
  23.8 3.1 copy-start.29
  23.8 5.7 copy-start.17
  26.9 9.6 copy-start.5
  168.8 2.9 copy-start.15
  387.1 2.9 copy-start.15
  532.6 2.9 copy-start.15
  605.4 3.0 copy-start.15
  688.6 17.2 copy-start.26
  688.6 17.2 copy-start.28
  706.5 8.0 copy-start.8
  709.6 4.9 copy-start.10
  709.7 2.8 collective-permute-start.4
  711.0 13.6 copy-start.23
  711.0 3.6 collective-permute-start.5
  714.6 10.2 copy-start.6
  715.4 47.6 %collective-permute-start.6 = (bf16[2,32,18,1,128]{4,1,3,2,0:T(8,128)(2,1)}, bf16[2,32,18,1,128]{4,1,3,2,0:T(8,128)(2,1)}, u32[]{:S(2)}, u32[]{:S(2)}) collective-permute-start(bf16[2,32,18,1,128]{4,1,3,2,0:T(8,128)(2,1)} %get-tuple-element.429), channel_id=1, source_target_pairs={{0,1},{1,2},{2,3},{4,5},{5,6},{6,7},{8,9},{9,10},{10,11},{12,13},{... | collective-permute-start | bytes 884744 | tf_op jit(solution)/shard_map/ppermute | solution.py:15
  723.3 39.7 %collective-permute-start.7 = (bf16[2,32,18,1,128]{4,1,3,2,0:T(8,128)(2,1)S(1)}, bf16[2,32,18,1,128]{4,1,3,2,0:T(8,128)(2,1)}, u32[]{:S(2)}, u32[]{:S(2)}) collective-permute-start(bf16[2,32,18,1,128]{4,1,3,2,0:T(8,128)(2,1)S(1)} %get-tuple-element.430), channel_id=1, source_target_pairs={{1,0},{2,1},{3,2},{5,4},{6,5},{7,6},{9,8},{10,9},{11,10},{13,12},{... | collective-permute-start | bytes 884744 | tf_op jit(solution)/shard_map/ppermute | solution.py:16
  759.1 3.9 copy-start.9
  759.1 3.9 copy-start.11
  856.4 3.3 copy-start.25
  892.3 4.3 copy-start.1
  932.6 4.8 copy-start.13
  976.2 3.1 copy-start.25
  1012.0 4.3 copy-start.1
  1052.2 4.7 copy-start.13
  1095.9 3.1 copy-start.25
  1131.6 4.3 copy-start.1
  1171.9 4.7 copy-start.13
  1215.5 3.1 copy-start.25
  1251.3 4.3 copy-start.1
  1291.5 4.7 copy-start.13
  1335.0 3.1 copy-start.25
  1370.8 4.3 copy-start.1
  1411.1 4.7 copy-start.13
  1454.6 3.1 copy-start.25
  1490.4 4.3 copy-start.1
  1530.7 4.8 copy-start.13
  1574.2 3.1 copy-start.25
  1610.0 4.3 copy-start.1
  1650.3 4.8 copy-start.13
  1693.3 3.1 copy-start.25
  1729.1 4.3 copy-start.1
  1769.3 4.7 copy-start.13
  1783.0 23.0 copy-start.20
  1833.8 10.5 collective-permute-start.8
  1835.1 9.2 collective-permute-start.9
  1844.4 141.4 %collective-permute-start.10 = (bf16[1,32,18,1,128]{4,1,3,2,0:T(8,128)(2,1)S(1)}, bf16[1,32,18,1,128]{4,1,3,2,0:T(8,128)(2,1)S(1)}, u32[]{:S(2)}, u32[]{:S(2)}) collective-permute-start(bf16[1,32,18,1,128]{4,1,3,2,0:T(8,128)(2,1)S(1)} %get-tuple-element.433), channel_id=1, source_target_pairs={{0,1},{1,2},{2,3},{4,5},{5,6},{6,7},{8,9},{9,10},{10,11},{12,13},{... | collective-permute-start | bytes 442376 | tf_op jit(solution)/shard_map/ppermute | solution.py:15
  1847.7 138.1 %collective-permute-start.11 = (bf16[1,32,18,1,128]{4,1,3,2,0:T(8,128)(2,1)S(1)}, bf16[1,32,18,1,128]{4,1,3,2,0:T(8,128)(2,1)S(1)}, u32[]{:S(2)}, u32[]{:S(2)}) collective-permute-start(bf16[1,32,18,1,128]{4,1,3,2,0:T(8,128)(2,1)S(1)} %get-tuple-element.434), channel_id=1, source_target_pairs={{1,0},{2,1},{3,2},{5,4},{6,5},{7,6},{9,8},{10,9},{11,10},{13,12},{... | collective-permute-start | bytes 442376 | tf_op jit(solution)/shard_map/ppermute | solution.py:16
  1985.8 8.2 copy-start.7
  2058.2 5.1 copy-start
  2097.8 5.1 copy-start
  2137.4 5.1 copy-start
  2176.9 5.1 copy-start
  2216.5 5.1 copy-start
  2256.0 5.1 copy-start
  2295.6 5.1 copy-start
  2334.7 5.1 copy-start
  (63 other events, 85.7 us)
Sparse Core Ops, SparseCore 0:
  1844.4 139.1 all-reduce.19
where the time goes:
time: 2390 us; the launch traced here: 2360 us
  matrix products  934 us (39%)
  local copies, waits for them, and re-layouts  918 us (38%)
  other arithmetic  239 us (10%)
  waiting for transfers between devices  142 us (6%)
  loops' own time  83.2 us (3%)
  starting transfers between devices  27.6 us (1%)
    dot_general x864, matrix products, convolve(): jnp.dot(kernel[number], window[:, offset:offset + length], preferred_elem...  639 us
    dot_general x432, matrix products, weight_gradient(): lax.dot_general(grid, window[:, offset:offset + length], (((1,), (1,)), (...  296 us
    reshape x56, local copies, waits for them, and re-layouts, grid_to_brick(): padded.reshape(channels, brick_edge, window_edge, window_edge)  169 us
    while x8, local copies, waits for them, and re-layouts, own_pass(): lax.fori_loop(0, own_count, visit, (initial, jnp.zeros(grad_shape, jnp.fl...  153 us
    psum x1, waiting for transfers between devices, local(): lax.psum((first_partial, second_partial), ('depth', 'group'))  135 us
    pad x56, local copies, waits for them, and re-layouts, grid_to_brick(): padded = jnp.pad(values, ((0, 0), (0, full_size - values.shape[1])))  84.9 us
    another operation x3, loops' own time, own_pass(): lax.fori_loop(0, own_count, visit, (initial, jnp.zeros(grad_shape, jnp.fl...  83.2 us
    slice x8, local copies, waits for them, and re-layouts, second_round(): windows[2]  71 us
  transfers between devices with their start and end apart: 13, of which 4 were waited for; matrix products, arithmetic and copies ran while one was open for 2% of the time, Pallas kernels for 0%

commit v1 on v0

--- a/solution.py
+++ b/solution.py
@@ -3,6 +3,11 @@
 import jax.numpy as jnp
 from jax import lax
 from jax.sharding import PartitionSpec as P
+
+
+def by_each_axis(x, axis_one, axis_two):
+    half = lax.psum(x, axis_one)
+    return lax.psum(half, axis_two)
 
 
 def extended_2(shard, sides, width):
@@ -225,7 +230,7 @@
         padded, cotangent_two[None], lambda windows: third_round(windows, kernels, brick_edge)
     )
     input_grad_two = third_stack[0]
-    first_total, second_total = lax.psum((first_partial, second_partial), ("depth", "group"))
+    first_total, second_total = by_each_axis((first_partial, second_partial), "group", "depth")
     scale = 1.0 / math.sqrt(
         float(brick_edge * lax.axis_size("depth") * brick_edge * groups * across)
     )

time: 2390 us -> 2300 us (0.962)
  waiting for transfers between devices: 142 us -> 56.4 us
    psum x1 -> x2, waiting for transfers between devices: 135 us -> 48.5 us  [the longest x1 48.5 us: by_each_axis(): half = lax.psum(x, axis_one)]
  transfers between devices with their start and end apart: 13 -> 14, of which waited for: 4 -> 4; matrix products, arithmetic and copies ran while one was open for 2% -> 19% of each run, Pallas kernels for 0% -> 0%
where the time goes in v1:
time: 2300 us; the launch traced here: 2270 us
  matrix products  934 us (41%)
  local copies, waits for them, and re-layouts  919 us (40%)
  other arithmetic  239 us (10%)
  loops' own time  81.6 us (4%)
  waiting for transfers between devices  56.4 us (2%)
  starting transfers between devices  25.8 us (1%)
    dot_general x864, matrix products, convolve(): jnp.dot(kernel[number], window[:, offset:offset + length], preferred_elem...  639 us
    dot_general x432, matrix products, weight_gradient(): lax.dot_general(grid, window[:, offset:offset + length], (((1,), (1,)), (...  296 us
    reshape x56, local copies, waits for them, and re-layouts, grid_to_brick(): padded.reshape(channels, brick_edge, window_edge, window_edge)  169 us
    while x8, local copies, waits for them, and re-layouts, own_pass(): lax.fori_loop(0, own_count, visit, (initial, jnp.zeros(grad_shape, jnp.fl...  154 us
    pad x56, local copies, waits for them, and re-layouts, grid_to_brick(): padded = jnp.pad(values, ((0, 0), (0, full_size - values.shape[1])))  84.8 us
    another operation x3, loops' own time, own_pass(): lax.fori_loop(0, own_count, visit, (initial, jnp.zeros(grad_shape, jnp.fl...  81.6 us
    slice x8, local copies, waits for them, and re-layouts, second_round(): windows[2]  71.1 us
    dynamic_update_slice x24, other arithmetic, visit(): lax.dynamic_update_slice(slab_stack, cubes, (anchor, anchor, anchor, anch...  66.9 us
  transfers between devices with their start and end apart: 14, of which 4 were waited for; matrix products, arithmetic and copies ran while one was open for 19% of the time, Pallas kernels for 0%

profile of v1, /device:TPU:0, one launch (start us, length us, event | category | flops | bytes accessed | tf_op | source)
XLA Modules:
  0.0 2270.8 jit_solution(11013892018252633689)
XLA Ops:
  29.5 6.9 select_maximum_fusion.6
  36.4 9.6 fusion.928
  46.0 22.5 copy.67
  68.5 6.4 broadcast.173
  75.7 612.5 %while.40 = (s32[]{:T(128)}, bf16[2,32,16,16,128]{1,4,3,2,0:T(8,128)(2,1)}, f32[27,32,32]{2,1,0:T(8,128)}, s32[]{:T(128)}, s32[8]{0:T(128)S(1)}, /*index=5*/bf16...) while((s32[]{:T(128)}, ...), condition=%wide.region_3.4_spmd, body=%wide.region_2.3_spmd.sunk | while | flops 587555840 | bytes 164357712 | solution.py:176
  100.8 6.3 constant_dynamic-slice_fusion.10
  129.9 4.2 reshape.203
  173.6 6.4 constant_dynamic-slice_fusion.10
  246.3 6.3 constant_dynamic-slice_fusion.10
  319.0 6.3 constant_dynamic-slice_fusion.10
  391.7 6.4 constant_dynamic-slice_fusion.10
  464.5 6.3 constant_dynamic-slice_fusion.10
  537.2 6.3 constant_dynamic-slice_fusion.10
  610.0 5.9 constant_dynamic-slice_fusion.10
  688.2 15.1 copy.68
  715.0 7.9 collective-permute-start.6
  724.3 5.9 copy.79
  733.2 5.9 copy.84
  739.1 17.1 stack.360.clone
  762.6 14.0 select_maximum_fusion
  776.6 6.9 fusion.920
  783.5 33.0 %copy.72 = bf16[3,32,18,18,130]{1,4,3,2,0:T(8,128)(2,1)} copy(bf16[3,32,18,18,130]{4,1,3,2,0:T(8,128)(2,1)} %fusion.920) | data formatting | bytes 16174080 | tf_op jit(solution)/shard_map/while | solution.py:176
  817.3 964.9 %while.41 = (s32[]{:T(128)}, bf16[3,32,16,16,128]{1,4,3,2,0:T(8,128)(2,1)}, f32[27,32,32]{2,1,0:T(8,128)}, s32[]{:T(128)}, s32[8]{0:T(128)S(1)}, /*index=5*/bf16...) while((s32[]{:T(128)}, ...), condition=%wide.region_5.6_spmd, body=%wide.region_4.5_spmd.sunk | while | flops 883973120 | bytes 240212160 | solution.py:176
  819.4 9.0 constant_dynamic-slice_fusion.11
  891.9 4.3 reshape.208
  901.5 4.9 fusion.1743
  939.2 9.0 constant_dynamic-slice_fusion.11
  1011.5 4.3 reshape.208
  1021.2 4.9 fusion.1743
  1058.7 9.0 constant_dynamic-slice_fusion.11
  1131.0 4.3 reshape.208
  1140.7 4.9 fusion.1743
  1178.3 9.0 constant_dynamic-slice_fusion.11
  1250.7 4.3 reshape.208
  1260.4 4.9 fusion.1743
  1297.9 8.9 constant_dynamic-slice_fusion.11
  1370.2 4.3 reshape.208
  1379.9 4.9 fusion.1743
  1417.4 8.9 constant_dynamic-slice_fusion.11
  1489.7 4.3 reshape.208
  1499.4 4.9 fusion.1743
  1537.0 8.9 constant_dynamic-slice_fusion.11
  1609.3 4.3 reshape.208
  1618.9 4.9 fusion.1743
  1656.6 8.3 constant_dynamic-slice_fusion.11
  1728.3 4.3 reshape.208
  1737.9 4.9 fusion.1743
  1782.2 22.0 copy.73
  1807.7 4.4 fusion.937
  1814.2 24.2 %copy.74 = bf16[3,32,16,16,128]{4,3,2,1,0:T(8,128)(2,1)} copy(bf16[3,32,16,16,128]{1,4,3,2,0:T(8,128)(2,1)} %get-tuple-element.288) | data formatting | bytes 12582912 | tf_op jit(solution)/shard_map/while | solution.py:176
  1846.9 48.5 %all-reduce.24.cloned.1.call-done = (f32[27,32,32]{2,1,0:T(8,128)}, f32[27,32,32]{2,1,0:T(8,128)}) async-done(((f32[27,32,32]{2,1,0:T(8,128)}, f32[27,32,32]{2,1,0:T(8,128)}), (f32[27,32,32]{2,1,0:T(8,128)}, f32[27,32,32]{2,1,0:T(8,128)})) %all-reduce.24.cloned.1.call-update) | async-done | bytes 221200 | tf_op jit(solution)/shard_map/psum | solution.py:9
  1895.5 8.2 select_maximum_fusion.2
  1903.6 9.6 fusion.929
  1913.2 22.5 copy.80
  1935.8 317.0 %while.42 = (s32[]{:T(128)}, bf16[1,32,16,16,128]{1,4,3,2,0:T(8,128)(2,1)}, s32[]{:T(128)}, s32[8]{0:T(128)S(1)}, bf16[2,32,18,18,130]{1,4,3,2,0:T(8,128)(2,1)},...) while((s32[]{:T(128)}, ...), condition=%wide.region_7.8_spmd, body=%wide.region_6.7_spmd.sunk | while | flops 295106560 | bytes 87847184 | solution.py:176
  1937.9 6.3 constant_dynamic-slice_fusion.12
  1977.4 6.4 constant_dynamic-slice_fusion.12
  2017.0 6.3 constant_dynamic-slice_fusion.12
  2056.5 6.3 constant_dynamic-slice_fusion.12
  2096.0 6.4 constant_dynamic-slice_fusion.12
  2135.6 6.3 constant_dynamic-slice_fusion.12
  2175.1 6.3 constant_dynamic-slice_fusion.12
  2214.7 5.9 constant_dynamic-slice_fusion.12
  2252.8 8.6 copy.81
  (1908 shorter events, 1625.6 us)
Async XLA Ops:
  7.2 1888.2 %all-reduce.24.cloned.1.call-start = ((), (), s32[]{:S(2)}) async-start(), calls=%async_computation.1 | async-start | bytes 1769472 | tf_op jit(solution)/shard_map/psum | solution.py:9
  8.2 3.0 copy-start.27
  11.1 7.8 copy-start.16
  11.2 3.7 collective-permute-start
  13.6 5.3 collective-permute-start.1
  19.0 8.8 collective-permute-start.2
  22.5 7.0 collective-permute-start.3
  23.8 3.1 copy-start.29
  23.8 5.7 copy-start.17
  26.9 9.5 copy-start.5
  605.1 3.0 copy-start.15
  688.2 17.2 copy-start.26
  688.2 17.2 copy-start.28
  706.1 8.0 copy-start.8
  709.2 4.9 copy-start.10
  709.3 2.8 collective-permute-start.4
  710.6 13.6 copy-start.23
  710.6 3.6 collective-permute-start.5
  714.2 10.2 copy-start.6
  715.0 47.6 %collective-permute-start.6 = (bf16[2,32,18,1,128]{4,1,3,2,0:T(8,128)(2,1)}, bf16[2,32,18,1,128]{4,1,3,2,0:T(8,128)(2,1)}, u32[]{:S(2)}, u32[]{:S(2)}) collective-permute-start(bf16[2,32,18,1,128]{4,1,3,2,0:T(8,128)(2,1)} %get-tuple-element.431), channel_id=1, source_target_pairs={{0,1},{1,2},{2,3},{4,5},{5,6},{6,7},{8,9},{9,10},{10,11},{12,13},{... | collective-permute-start | bytes 884744 | tf_op jit(solution)/shard_map/ppermute | solution.py:20
  722.9 39.7 %collective-permute-start.7 = (bf16[2,32,18,1,128]{4,1,3,2,0:T(8,128)(2,1)S(1)}, bf16[2,32,18,1,128]{4,1,3,2,0:T(8,128)(2,1)}, u32[]{:S(2)}, u32[]{:S(2)}) collective-permute-start(bf16[2,32,18,1,128]{4,1,3,2,0:T(8,128)(2,1)S(1)} %get-tuple-element.432), channel_id=1, source_target_pairs={{1,0},{2,1},{3,2},{5,4},{6,5},{7,6},{9,8},{10,9},{11,10},{13,12},{... | collective-permute-start | bytes 884744 | tf_op jit(solution)/shard_map/ppermute | solution.py:21
  758.7 3.9 copy-start.9
  758.7 3.9 copy-start.11
  856.0 3.3 copy-start.25
  891.9 4.3 copy-start.1
  932.1 4.8 copy-start.13
  975.7 3.1 copy-start.25
  1011.5 4.3 copy-start.1
  1051.7 4.7 copy-start.13
  1095.3 3.1 copy-start.25
  1131.0 4.3 copy-start.1
  1171.3 4.7 copy-start.13
  1214.9 3.1 copy-start.25
  1250.7 4.3 copy-start.1
  1290.9 4.7 copy-start.13
  1334.4 3.1 copy-start.25
  1370.2 4.3 copy-start.1
  1410.4 4.7 copy-start.13
  1453.9 3.1 copy-start.25
  1489.7 4.3 copy-start.1
  1529.9 4.8 copy-start.13
  1573.5 3.1 copy-start.25
  1609.3 4.3 copy-start.1
  1649.5 4.8 copy-start.13
  1692.5 3.1 copy-start.25
  1728.3 4.3 copy-start.1
  1768.5 4.7 copy-start.13
  1782.1 25.6 %copy-start.20 = (bf16[32,16,16,128]{3,2,1,0:T(8,128)(2,1)S(1)}, bf16[32,16,16,128]{3,2,1,0:T(8,128)(2,1)}, u32[]{:S(2)}) copy-start(bf16[32,16,16,128]{3,2,1,0:T(8,128)(2,1)} %param.13) | copy-start | bytes 6291460
  1805.1 33.3 %collective-permute-start.8 = (bf16[1,32,1,16,128]{4,1,3,2,0:T(8,128)(2,1)S(1)}, bf16[1,32,1,16,128]{4,1,3,2,0:T(8,128)(2,1)S(1)}, u32[]{:S(2)}, u32[]{:S(2)}) collective-permute-start(bf16[1,32,1,16,128]{4,1,3,2,0:T(8,128)(2,1)S(1)} %get-tuple-element.429), channel_id=1, source_target_pairs={{0,4},{4,8},{8,12},{12,16},{16,20},{20,24},{24,28},{1,5},{5,9},{9,... | collective-permute-start | bytes 393224 | tf_op jit(solution)/shard_map/ppermute | solution.py:20
  1806.4 32.0 %collective-permute-start.9 = (bf16[1,32,1,16,128]{4,1,3,2,0:T(8,128)(2,1)S(1)}, bf16[1,32,1,16,128]{4,1,3,2,0:T(8,128)(2,1)S(1)}, u32[]{:S(2)}, u32[]{:S(2)}) collective-permute-start(bf16[1,32,1,16,128]{4,1,3,2,0:T(8,128)(2,1)S(1)} %get-tuple-element.430), channel_id=1, source_target_pairs={{4,0},{8,4},{12,8},{16,12},{20,16},{24,20},{28,24},{5,1},{9,5},{13... | collective-permute-start | bytes 393224 | tf_op jit(solution)/shard_map/ppermute | solution.py:21
  1814.1 24.3 %copy-start.18 = (bf16[1,32,16,16,128]{4,1,3,2,0:T(8,128)(2,1)}, bf16[1,32,16,16,128]{4,1,3,2,0:T(8,128)(2,1)S(1)}, u32[]{:S(2)}) copy-start(bf16[1,32,16,16,128]{4,1,3,2,0:T(8,128)(2,1)S(1)} %slice.1760) | copy-start | bytes 6291460
  1838.4 423.0 %all-reduce.22.cloned.1.call-start = ((), (), s32[]{:S(2)}) async-start(), calls=%async_computation | async-start | bytes 1769472 | tf_op jit(solution)/shard_map/psum | solution.py:10
  1838.5 56.9 %collective-permute-start.10 = (bf16[1,32,18,1,128]{4,1,3,2,0:T(8,128)(2,1)S(1)}, bf16[1,32,18,1,128]{4,1,3,2,0:T(8,128)(2,1)S(1)}, u32[]{:S(2)}, u32[]{:S(2)}) collective-permute-start(bf16[1,32,18,1,128]{4,1,3,2,0:T(8,128)(2,1)S(1)} %get-tuple-element.435), channel_id=1, source_target_pairs={{0,1},{1,2},{2,3},{4,5},{5,6},{6,7},{8,9},{9,10},{10,11},{12,13},{... | collective-permute-start | bytes 442376 | tf_op jit(solution)/shard_map/ppermute | solution.py:20
  1839.8 4.9 copy-start.21
  1839.8 55.6 %collective-permute-start.11 = (bf16[1,32,18,1,128]{4,1,3,2,0:T(8,128)(2,1)S(1)}, bf16[1,32,18,1,128]{4,1,3,2,0:T(8,128)(2,1)S(1)}, u32[]{:S(2)}, u32[]{:S(2)}) collective-permute-start(bf16[1,32,18,1,128]{4,1,3,2,0:T(8,128)(2,1)S(1)} %get-tuple-element.436), channel_id=1, source_target_pairs={{1,0},{2,1},{3,2},{5,4},{6,5},{7,6},{9,8},{10,9},{11,10},{13,12},{... | collective-permute-start | bytes 442376 | tf_op jit(solution)/shard_map/ppermute | solution.py:21
  1895.4 8.2 copy-start.7
  1967.9 5.1 copy-start
  2007.5 5.1 copy-start
  2047.0 5.1 copy-start
  2086.6 5.1 copy-start
  2126.1 5.1 copy-start
  2165.7 5.1 copy-start
  2205.2 5.1 copy-start
  2244.3 5.1 copy-start
  (64 other events, 90.0 us)
Sparse Core Ops, SparseCore 0:
  1838.5 56.8 all-reduce.23
  1898.7 55.1 all-reduce.21
